TPU v7x, 512 devices: a whole 4x8x8 slice. The times are simulated.
512 devices in a mesh: ao: 32 (over x, z), ri: 16 (over y, core).
Axes of the slice: x: 4, y: 8, z: 8, core: 2. Of those that a mesh axis runs over, the one named last changes fastest.
Arguments:
- three_center: bfloat16 [256, 12288, 128], P('ri', 'ao'), may hold values from -0.19921875 to 0.19921875
- occ_band: bfloat16 [4096, 640], P('ao'), may hold values from -0.3125 to 0.3125
- virt_band: bfloat16 [4096, 384], P('ao'), may hold values from -0.3125 to 0.3125
- three_mask: int32 [32, 3], P('ao'), may hold values 0 or 1
- occ_mask: int32 [32, 5], P('ao'), may hold values 0 or 1
- virt_mask: int32 [32, 3], P('ao'), may hold values 0 or 1
Outputs:
- chi: float32 [256, 256], P('ri')
All inputs are finite; a program needn't handle non-finite values. No bound on the sum of `three_mask` or of `occ_mask` or of `virt_mask` on one device may be relied on, other than what follows from the above.
Results may differ from a plain program's by a relative error of at most 0.004.
Values may be sent and summed in bfloat16 or wider, within the bound.
A program may use at most 64 MiB of HBM per device.

v0:
```python
import jax
import jax.numpy as jnp
from jax import lax
from jax.sharding import PartitionSpec as P


def padded_2(value, sides, width):
    for axis, dim in sides:
        peers, length = (lax.axis_size(axis), value.shape[dim])
        up = [(i, (i + 1) % peers) for i in range(peers)]
        down = [(j, i) for i, j in up]
        last = lax.slice_in_dim(value, length - width, length, axis=dim)
        initial = lax.slice_in_dim(value, 0, width, axis=dim)
        before = lax.ppermute(last, axis, up)
        after = lax.ppermute(initial, axis, down)
        value = jnp.concatenate([before, value, after], axis=dim)
    return value


def per_device(three_center, occ_band, virt_band, three_mask, occ_mask, virt_mask):
    tile_size = occ_band.shape[0]
    local_rows = three_center.shape[0]
    live_b = (
        three_center.reshape(local_rows, 3, tile_size, tile_size)
        * three_mask[0].astype(three_center.dtype)[None, :, None, None]
    )
    live_b = live_b.reshape(local_rows, 3 * tile_size, tile_size)
    live_occ = occ_band * jnp.repeat(occ_mask[0].astype(occ_band.dtype), tile_size)[None, :]
    live_virt = virt_band * jnp.repeat(virt_mask[0].astype(virt_band.dtype), tile_size)[None, :]
    occ_rows = padded_2(live_occ, (("ao", 0),), tile_size)
    blank = jnp.zeros((tile_size, tile_size), occ_band.dtype)
    green_block = jnp.concatenate(
        [
            jnp.concatenate([occ_rows[0:tile_size, tile_size:], blank], 1),
            occ_rows[tile_size : 2 * tile_size],
            jnp.concatenate([blank, occ_rows[2 * tile_size :, : 4 * tile_size]], 1),
        ],
        0,
    )
    m_local = jnp.einsum(
        "ml,pmn->pln", green_block, live_b, preferred_element_type=jnp.float32
    ).astype(jnp.bfloat16)
    padded = padded_2(m_local, (("ao", 2),), tile_size)
    needed = jnp.concatenate(
        [
            padded[:, 2 * tile_size : 5 * tile_size, 0:tile_size],
            padded[:, tile_size : 4 * tile_size, tile_size : 2 * tile_size],
            padded[:, 0 : 3 * tile_size, 2 * tile_size : 3 * tile_size],
        ],
        2,
    )
    product = jnp.einsum(
        "plv,sv->pls", needed, live_virt, preferred_element_type=jnp.float32
    ).astype(jnp.bfloat16)
    product_flat = product.reshape(local_rows, 3 * tile_size * tile_size)
    b_flat = live_b.reshape(local_rows, 3 * tile_size * tile_size)
    product_all, b_all = (
        lax.all_to_all(product_flat, "ri", split_axis=1, concat_axis=0, tiled=True),
        lax.all_to_all(b_flat, "ri", split_axis=1, concat_axis=0, tiled=True),
    )
    partial_chi = lax.dot_general(
        product_all, b_all, (((1,), (1,)), ((), ())), preferred_element_type=jnp.float32
    )
    row_panel = lax.psum_scatter(partial_chi, "ri", scatter_dimension=0, tiled=True)
    summed = lax.psum(row_panel, "ao")
    return -summed


def solution(mesh):
    placed = (
        P("ri", "ao", None),
        P("ao", None),
        P("ao", None),
        P("ao", None),
        P("ao", None),
        P("ao", None),
    )
    return jax.shard_map(
        per_device, mesh=mesh, in_specs=placed, out_specs=P("ri", None), check_vma=False
    )
```

profile of v0, /device:TPU:32, one launch (start us, length us, event | category | flops | bytes accessed | tf_op | source)
XLA Modules:
  0.0 353.9 jit_solution(3540133267525671056)
XLA Ops:
  6.5 0.7 convert_bitcast_fusion.2
  7.3 0.9 broadcast_multiply_fusion.1
  8.2 4.3 %collective-permute-start = (bf16[128,640]{1,0:T(8,128)(2,1)S(1)}, bf16[128,640]{1,0:T(8,128)(2,1)}, u32[]{:S(2)}, u32[]{:S(2)}) collective-permute-start(bf16[128,640]{1,0:T(8,128)(2,1)S(1)} %broadcast_multiply_fusion.1), channel_id=1, source_target_pairs={{0,16},{16,32},{32,48},{48,64},{64,80},{80,96},{96,112},{112,128},... | collective-permute-start | bytes 491528 | tf_op jit(solution)/shard_map/ppermute | solution.py:14
  12.5 10.8 %collective-permute-start.1 = (bf16[128,640]{1,0:T(8,128)(2,1)S(1)}, bf16[128,640]{1,0:T(8,128)(2,1)}, u32[]{:S(2)}, u32[]{:S(2)}) collective-permute-start(bf16[128,640]{1,0:T(8,128)(2,1)S(1)} %broadcast_multiply_fusion.1), channel_id=1, source_target_pairs={{16,0},{32,16},{48,32},{64,48},{80,64},{96,80},{112,96},{128,112},... | collective-permute-start | bytes 491528 | tf_op jit(solution)/shard_map/ppermute | solution.py:15
  23.3 0.7 convert_bitcast_fusion.3
  24.1 2.7 reshape.31
  26.9 0.9 slice.20
  27.8 0.9 slice.21
  28.7 3.3 convert_bitcast_fusion
  32.0 1.9 collective-permute-start.2
  34.0 7.2 %collective-permute-start.3 = (bf16[16,640,128]{1,2,0:T(8,128)(2,1)}, bf16[16,640,128]{1,2,0:T(8,128)(2,1)}, u32[]{:S(2)}, u32[]{:S(2)}) collective-permute-start(bf16[16,640,128]{1,2,0:T(8,128)(2,1)} %convert_bitcast_fusion), channel_id=1, source_target_pairs={{16,0},{32,16},{48,32},{64,48},{80,64},{96,80},{112,96},{128,112},... | collective-permute-start | bytes 7864328 | tf_op jit(solution)/shard_map/ppermute | solution.py:15
  41.3 2.0 copy.19
  43.4 7.4 %all-to-all-start.1 = ((bf16[16,16,3072]{2,0,1:T(8,128)(2,1)}), bf16[16,16,3072]{2,0,1:T(8,128)(2,1)}, u32[]{:S(2)}, u32[]{:S(2)}) async-start(bf16[16,16,3072]{2,0,1:T(8,128)(2,1)} %copy.19), calls=%async_computation.1 | async-start | bytes 3145728 | tf_op jit(solution)/shard_map/all_to_all | solution.py:59
  50.9 1.6 slice.23
  52.5 43.4 %collective-permute-done.2 = bf16[16,640,128]{1,2,0:T(8,128)(2,1)} collective-permute-done((bf16[16,640,128]{1,2,0:T(8,128)(2,1)}, bf16[16,640,128]{1,2,0:T(8,128)(2,1)}, u32[]{:S(2)}, u32[]{:S(2)}) %collective-permute-start.2) | collective-permute-done | bytes 2621472 | tf_op jit(solution)/shard_map/ppermute | solution.py:14
  95.9 1.6 slice.22
  97.5 1.6 slice.24
  99.2 1.7 fusion.6
  100.8 0.7 all_to_all.26
  101.5 0.9 copy.18
  102.4 42.5 %all_to_all.35 = bf16[16,16,3072]{2,0,1:T(8,128)(2,1)S(1)} all-to-all(bf16[16,16,3072]{2,0,1:T(8,128)(2,1)S(1)} %copy.18), channel_id=1, replica_groups=mesh['ao'=32,'ri'=16] {'ri'}, dimensions={1} | all-to-all | bytes 3145728 | tf_op jit(solution)/shard_map/all_to_all | solution.py:58
  144.9 2.7 fusion.32
  147.6 55.1 %reduce-scatter.2.cloned.1.call-done = f32[16,256]{1,0:T(8,128)} async-done(((f32[256,256]{1,0:T(8,128)}), f32[16,256]{1,0:T(8,128)}) %reduce-scatter.2.cloned.1.call-update) | async-done | bytes 16400 | tf_op jit(solution)/shard_map/reduce_scatter | solution.py:64
  202.8 143.7 %psum.7 = f32[16,256]{1,0:T(8,128)S(1)} all-reduce(f32[16,256]{1,0:T(8,128)} %reduce-scatter.2.cloned.1.call-done), channel_id=1, replica_groups=mesh['ao'=32,'ri'=16] {'ao'}, use_global_device_ids=true, to_apply=%region_1.0 | all-reduce | flops 4096 | bytes 32768 | tf_op jit(solution)/shard_map/psum | solution.py:65
  (20 shorter events, 1.2 us)
Async XLA Ops:
  8.2 18.7 %collective-permute-start = (bf16[128,640]{1,0:T(8,128)(2,1)S(1)}, bf16[128,640]{1,0:T(8,128)(2,1)}, u32[]{:S(2)}, u32[]{:S(2)}) collective-permute-start(bf16[128,640]{1,0:T(8,128)(2,1)S(1)} %broadcast_multiply_fusion.1), channel_id=1, source_target_pairs={{0,16},{16,32},{32,48},{48,64},{64,80},{80,96},{96,112},{112,128},... | collective-permute-start | bytes 491528 | tf_op jit(solution)/shard_map/ppermute | solution.py:14
  12.5 15.3 %collective-permute-start.1 = (bf16[128,640]{1,0:T(8,128)(2,1)S(1)}, bf16[128,640]{1,0:T(8,128)(2,1)}, u32[]{:S(2)}, u32[]{:S(2)}) collective-permute-start(bf16[128,640]{1,0:T(8,128)(2,1)S(1)} %broadcast_multiply_fusion.1), channel_id=1, source_target_pairs={{16,0},{32,16},{48,32},{64,48},{80,64},{96,80},{112,96},{128,112},... | collective-permute-start | bytes 491528 | tf_op jit(solution)/shard_map/ppermute | solution.py:15
  24.1 4.6 %copy-start = (bf16[16,384,128]{2,1,0:T(8,128)(2,1)S(1)}, bf16[16,384,128]{2,1,0:T(8,128)(2,1)}, u32[]{:S(2)}) copy-start(bf16[16,384,128]{2,1,0:T(8,128)(2,1)} %param.6) | copy-start | bytes 4718596
  32.0 63.8 %collective-permute-start.2 = (bf16[16,640,128]{1,2,0:T(8,128)(2,1)}, bf16[16,640,128]{1,2,0:T(8,128)(2,1)}, u32[]{:S(2)}, u32[]{:S(2)}) collective-permute-start(bf16[16,640,128]{1,2,0:T(8,128)(2,1)} %convert_bitcast_fusion), channel_id=1, source_target_pairs={{0,16},{16,32},{32,48},{48,64},{64,80},{80,96},{96,112},{112,128},... | collective-permute-start | bytes 7864328 | tf_op jit(solution)/shard_map/ppermute | solution.py:14
  34.0 63.5 %collective-permute-start.3 = (bf16[16,640,128]{1,2,0:T(8,128)(2,1)}, bf16[16,640,128]{1,2,0:T(8,128)(2,1)}, u32[]{:S(2)}, u32[]{:S(2)}) collective-permute-start(bf16[16,640,128]{1,2,0:T(8,128)(2,1)} %convert_bitcast_fusion), channel_id=1, source_target_pairs={{16,0},{32,16},{48,32},{64,48},{80,64},{96,80},{112,96},{128,112},... | collective-permute-start | bytes 7864328 | tf_op jit(solution)/shard_map/ppermute | solution.py:15
  43.4 7.4 %copy-start.2 = (s32[1,3]{1,0:T(1,128)S(1)}, s32[1,3]{1,0:T(1,128)}, u32[]{:S(2)}) copy-start(s32[1,3]{1,0:T(1,128)} %param.11) | copy-start | bytes 40
  43.4 59.0 %all-to-all-start.1 = ((bf16[16,16,3072]{2,0,1:T(8,128)(2,1)}), bf16[16,16,3072]{2,0,1:T(8,128)(2,1)}, u32[]{:S(2)}, u32[]{:S(2)}) async-start(bf16[16,16,3072]{2,0,1:T(8,128)(2,1)} %copy.19), calls=%async_computation.1 | async-start | bytes 3145728 | tf_op jit(solution)/shard_map/all_to_all | solution.py:59
  50.7 152.0 %reduce-scatter.2.cloned.1.call-start = ((), (), s32[]{:S(2)}) async-start(), calls=%async_computation.3 | async-start | bytes 278528 | tf_op jit(solution)/shard_map/reduce_scatter | solution.py:64
  97.5 1.7 copy-start.1
Sparse Core Ops, SparseCore 0:
  147.8 54.9 reduce-scatter.1
where the time goes:
time: 354 us
  blocking collectives  186 us (53%)
  waiting for transfers between devices  98.6 us (28%)
  starting transfers between devices  31.6 us (9%)
  between operations  13.6 us (4%)
  local copies, waits for them, and re-layouts  13.3 us (4%)
  matrix products  7.72 us (2%)
    psum x1, blocking collectives, per_device(): summed = lax.psum(row_panel, 'ao')  144 us
    reduce_scatter x1, waiting for transfers between devices, per_device(): lax.psum_scatter(partial_chi, 'ri', scatter_dimension=0, tiled=True)  55.1 us
    ppermute x2, waiting for transfers between devices, padded_2(): before = lax.ppermute(last, axis, up)  43.4 us
    all_to_all x1, blocking collectives, per_device(): lax.all_to_all(product_flat, 'ri', split_axis=1, concat_axis=0, tiled=True)  42.5 us
    ppermute x2, starting transfers between devices, padded_2(): after = lax.ppermute(initial, axis, down)  18 us
    all_to_all x1, starting transfers between devices, per_device(): lax.all_to_all(b_flat, 'ri', split_axis=1, concat_axis=0, tiled=True)  7.36 us
  transfers between devices with their start and end apart: 6, of which 2 were waited for; matrix products, arithmetic and copies ran while one was open for 4% of the time, Pallas kernels for 0%

commit v1 on v0

--- a/solution.py
+++ b/solution.py
@@ -1,7 +1,20 @@
+import functools
 import jax
 import jax.numpy as jnp
 from jax import lax
 from jax.sharding import PartitionSpec as P
+from jax.lax import all_to_all, axis_size
+
+
+def _enter_yards(obj, which_axis):
+    piece_next = axis_size(which_axis)
+    parts_out = jnp.split(obj, piece_next, axis=1)
+    current_value = jnp.stack(parts_out)
+    base_arr = all_to_all(current_value, which_axis, 0, 0)
+    return jnp.concatenate(base_arr, axis=0)
+
+
+obtain_clusters = functools.partial(_enter_yards, which_axis="ri")
 
 
 def padded_2(value, sides, width):
@@ -55,7 +68,7 @@
     product_flat = product.reshape(local_rows, 3 * tile_size * tile_size)
     b_flat = live_b.reshape(local_rows, 3 * tile_size * tile_size)
     product_all, b_all = (
-        lax.all_to_all(product_flat, "ri", split_axis=1, concat_axis=0, tiled=True),
+        obtain_clusters(product_flat),
         lax.all_to_all(b_flat, "ri", split_axis=1, concat_axis=0, tiled=True),
     )
     partial_chi = lax.dot_general(

time: 354 us -> 352 us (level)
  local copies, waits for them, and re-layouts: 13.3 us -> 9.16 us
  transfers between devices with their start and end apart: 6 -> 6, of which waited for: 2 -> 4; matrix products, arithmetic and copies ran while one was open for 4% -> 3% of each run, Pallas kernels for 0% -> 0%
where the time goes in v1:
time: 352 us
  blocking collectives  186 us (53%)
  waiting for transfers between devices  100 us (28%)
  starting transfers between devices  32.1 us (9%)
  between operations  13.7 us (4%)
  local copies, waits for them, and re-layouts  9.16 us (3%)
  matrix products  7.85 us (2%)
    psum x1, blocking collectives, per_device(): summed = lax.psum(row_panel, 'ao')  144 us
    reduce_scatter x1, waiting for transfers between devices, per_device(): lax.psum_scatter(partial_chi, 'ri', scatter_dimension=0, tiled=True)  55.2 us
    ppermute x2, waiting for transfers between devices, padded_2(): before = lax.ppermute(last, axis, up)  43.7 us
    all_to_all x1, blocking collectives, _enter_yards(): base_arr = all_to_all(current_value, which_axis, 0, 0)  42.5 us
    ppermute x2, starting transfers between devices, padded_2(): after = lax.ppermute(initial, axis, down)  18.5 us
    all_to_all x1, starting transfers between devices, per_device(): lax.all_to_all(b_flat, 'ri', split_axis=1, concat_axis=0, tiled=True)  7.36 us
  transfers between devices with their start and end apart: 6, of which 4 were waited for; matrix products, arithmetic and copies ran while one was open for 3% of the time, Pallas kernels for 0%

profile of v1, /device:TPU:32, one launch (start us, length us, event | category | flops | bytes accessed | tf_op | source)
XLA Modules:
  0.0 352.0 jit_solution(10024042779054979978)
XLA Ops:
  6.5 0.7 convert_bitcast_fusion.2
  7.3 0.9 broadcast_multiply_fusion.1
  8.2 4.3 %collective-permute-start = (bf16[128,640]{1,0:T(8,128)(2,1)S(1)}, bf16[128,640]{1,0:T(8,128)(2,1)S(1)}, u32[]{:S(2)}, u32[]{:S(2)}) collective-permute-start(bf16[128,640]{1,0:T(8,128)(2,1)S(1)} %broadcast_multiply_fusion.1), channel_id=1, source_target_pairs={{0,16},{16,32},{32,48},{48,64},{64,80},{80,96},{96,112},{112,128},... | collective-permute-start | bytes 491528 | tf_op jit(solution)/shard_map/ppermute | solution.py:27
  12.5 10.8 %collective-permute-start.1 = (bf16[128,640]{1,0:T(8,128)(2,1)S(1)}, bf16[128,640]{1,0:T(8,128)(2,1)S(1)}, u32[]{:S(2)}, u32[]{:S(2)}) collective-permute-start(bf16[128,640]{1,0:T(8,128)(2,1)S(1)} %broadcast_multiply_fusion.1), channel_id=1, source_target_pairs={{16,0},{32,16},{48,32},{64,48},{80,64},{96,80},{112,96},{128,112},... | collective-permute-start | bytes 491528 | tf_op jit(solution)/shard_map/ppermute | solution.py:28
  23.3 0.7 convert_bitcast_fusion.3
  24.0 1.5 collective-permute-done
  25.6 1.2 collective-permute-done.1
  26.7 4.9 %convert_bitcast_fusion = bf16[16,640,128]{1,2,0:T(8,128)(2,1)} fusion(bf16[16,384,128]{2,1,0:T(8,128)(2,1)} %param.6, bf16[384]{0:T(512)(128)(2,1)S(1)} %broadcast_bitcast_fusion.2, bf16[128,512]{1,0:T(8,128)(2,1)S(1)} %slice.21, bf16[128,512]{1,0:T(8,128)(2,1)S(1)} %slice.20, bf16[128,640]{1,0:T(8,128)(2,1)S(1)} %broadcast_multiply_fusion.1), kind=kOutput, calls=%fused_computation.6 | convolution fusion | flops 1011187712 | bytes 4621056 | tf_op jit(solution)/shard_map/ml,pmn->pln/dot_general | solution.py:53
  31.6 1.9 collective-permute-start.2
  33.5 7.7 %collective-permute-start.3 = (bf16[16,640,128]{1,2,0:T(8,128)(2,1)}, bf16[16,640,128]{1,2,0:T(8,128)(2,1)}, u32[]{:S(2)}, u32[]{:S(2)}) collective-permute-start(bf16[16,640,128]{1,2,0:T(8,128)(2,1)} %convert_bitcast_fusion), channel_id=1, source_target_pairs={{16,0},{32,16},{48,32},{64,48},{80,64},{96,80},{112,96},{128,112},... | collective-permute-start | bytes 7864328 | tf_op jit(solution)/shard_map/ppermute | solution.py:28
  41.2 0.7 reshape.34
  42.2 2.1 copy.16
  44.3 7.4 %all-to-all-start.1 = ((bf16[16,16,3072]{2,0,1:T(8,128)(2,1)}), bf16[16,16,3072]{2,0,1:T(8,128)(2,1)S(1)}, u32[]{:S(2)}, u32[]{:S(2)}) async-start(bf16[16,16,3072]{2,0,1:T(8,128)(2,1)} %copy.16), calls=%async_computation.1 | async-start | bytes 3145728 | tf_op jit(solution)/shard_map/all_to_all | solution.py:72
  51.8 1.6 slice.23
  53.4 42.2 %collective-permute-done.2 = bf16[16,640,128]{1,2,0:T(8,128)(2,1)} collective-permute-done((bf16[16,640,128]{1,2,0:T(8,128)(2,1)}, bf16[16,640,128]{1,2,0:T(8,128)(2,1)}, u32[]{:S(2)}, u32[]{:S(2)}) %collective-permute-start.2) | collective-permute-done | bytes 2621472 | tf_op jit(solution)/shard_map/ppermute | solution.py:27
  95.6 1.6 slice.22
  97.2 1.6 slice.24
  98.9 1.7 fusion.6
  100.5 1.0 copy.21
  101.8 42.5 %all_to_all.21 = bf16[16,16,3072]{2,1,0:T(8,128)(2,1)S(1)} all-to-all(bf16[16,16,3072]{2,1,0:T(8,128)(2,1)S(1)} %fusion.24), channel_id=1, replica_groups=mesh['ao'=32,'ri'=16] {'ri'}, dimensions={0} | all-to-all | bytes 3145728 | tf_op jit(solution)/shard_map/all_to_all | solution.py:13
  144.3 1.3 fusion.48
  145.7 55.2 %reduce-scatter.2.cloned.1.call-done = f32[16,256]{1,0:T(8,128)} async-done(((f32[256,256]{1,0:T(8,128)}), f32[16,256]{1,0:T(8,128)}) %reduce-scatter.2.cloned.1.call-update) | async-done | bytes 16400 | tf_op jit(solution)/shard_map/reduce_scatter | solution.py:77
  200.8 143.7 %psum.7 = f32[16,256]{1,0:T(8,128)S(1)} all-reduce(f32[16,256]{1,0:T(8,128)} %reduce-scatter.2.cloned.1.call-done), channel_id=1, replica_groups=mesh['ao'=32,'ri'=16] {'ao'}, use_global_device_ids=true, to_apply=%region_1.0 | all-reduce | flops 4096 | bytes 32768 | tf_op jit(solution)/shard_map/psum | solution.py:78
  344.5 0.6 neg.3
  (35 shorter events, 0.7 us)
Async XLA Ops:
  8.2 17.3 %collective-permute-start = (bf16[128,640]{1,0:T(8,128)(2,1)S(1)}, bf16[128,640]{1,0:T(8,128)(2,1)S(1)}, u32[]{:S(2)}, u32[]{:S(2)}) collective-permute-start(bf16[128,640]{1,0:T(8,128)(2,1)S(1)} %broadcast_multiply_fusion.1), channel_id=1, source_target_pairs={{0,16},{16,32},{32,48},{48,64},{64,80},{80,96},{96,112},{112,128},... | collective-permute-start | bytes 491528 | tf_op jit(solution)/shard_map/ppermute | solution.py:27
  12.5 14.2 %collective-permute-start.1 = (bf16[128,640]{1,0:T(8,128)(2,1)S(1)}, bf16[128,640]{1,0:T(8,128)(2,1)S(1)}, u32[]{:S(2)}, u32[]{:S(2)}) collective-permute-start(bf16[128,640]{1,0:T(8,128)(2,1)S(1)} %broadcast_multiply_fusion.1), channel_id=1, source_target_pairs={{16,0},{32,16},{48,32},{64,48},{80,64},{96,80},{112,96},{128,112},... | collective-permute-start | bytes 491528 | tf_op jit(solution)/shard_map/ppermute | solution.py:28
  26.7 14.5 %copy-start = (bf16[16,384,128]{2,1,0:T(8,128)(2,1)S(1)}, bf16[16,384,128]{2,1,0:T(8,128)(2,1)}, u32[]{:S(2)}) copy-start(bf16[16,384,128]{2,1,0:T(8,128)(2,1)} %param.6) | copy-start | bytes 4718596
  31.6 64.0 %collective-permute-start.2 = (bf16[16,640,128]{1,2,0:T(8,128)(2,1)}, bf16[16,640,128]{1,2,0:T(8,128)(2,1)}, u32[]{:S(2)}, u32[]{:S(2)}) collective-permute-start(bf16[16,640,128]{1,2,0:T(8,128)(2,1)} %convert_bitcast_fusion), channel_id=1, source_target_pairs={{0,16},{16,32},{32,48},{48,64},{64,80},{80,96},{96,112},{112,128},... | collective-permute-start | bytes 7864328 | tf_op jit(solution)/shard_map/ppermute | solution.py:27
  33.5 63.7 %collective-permute-start.3 = (bf16[16,640,128]{1,2,0:T(8,128)(2,1)}, bf16[16,640,128]{1,2,0:T(8,128)(2,1)}, u32[]{:S(2)}, u32[]{:S(2)}) collective-permute-start(bf16[16,640,128]{1,2,0:T(8,128)(2,1)} %convert_bitcast_fusion), channel_id=1, source_target_pairs={{16,0},{32,16},{48,32},{64,48},{80,64},{96,80},{112,96},{128,112},... | collective-permute-start | bytes 7864328 | tf_op jit(solution)/shard_map/ppermute | solution.py:28
  44.3 7.4 %copy-start.2 = (s32[1,3]{1,0:T(1,128)S(1)}, s32[1,3]{1,0:T(1,128)}, u32[]{:S(2)}) copy-start(s32[1,3]{1,0:T(1,128)} %param.11) | copy-start | bytes 40
  44.3 57.5 %all-to-all-start.1 = ((bf16[16,16,3072]{2,0,1:T(8,128)(2,1)}), bf16[16,16,3072]{2,0,1:T(8,128)(2,1)S(1)}, u32[]{:S(2)}, u32[]{:S(2)}) async-start(bf16[16,16,3072]{2,0,1:T(8,128)(2,1)} %copy.16), calls=%async_computation.1 | async-start | bytes 3145728 | tf_op jit(solution)/shard_map/all_to_all | solution.py:72
  51.7 149.1 %reduce-scatter.2.cloned.1.call-start = ((), (), s32[]{:S(2)}) async-start(), calls=%async_computation.3 | async-start | bytes 278528 | tf_op jit(solution)/shard_map/reduce_scatter | solution.py:77
  97.2 1.7 copy-start.1
Sparse Core Ops, SparseCore 0:
  145.8 54.9 reduce-scatter.1
